TPU v7x, 512 devices: a whole 4x8x8 slice. The times are simulated.
512 devices in a mesh: ctx: 64 (over x, y, core), head: 8 (over z).
Axes of the slice: x: 4, y: 8, z: 8, core: 2. Of those that a mesh axis runs over, the one named last changes fastest.
Arguments:
- placement: int32 [64], replicated, may hold values from 0 to 63, each once
- placed_queries: bfloat16 [16384, 4096], P('ctx', 'head'), may hold values from -160 to 160
- placed_keys: bfloat16 [16384, 1024], P('ctx', 'head'), may hold values from -4.5 to 4.5
- placed_values: bfloat16 [16384, 1024], P('ctx', 'head'), may hold values from -6 to 6
- out_weight: bfloat16 [4096, 4096], P('head', 'ctx'), may hold values from -0.25 to 0.25
Outputs:
- attention_out: bfloat16 [16384, 4096], P('ctx', 'head')
Inputs may be any that keep to these rules, and one draw needn't show every extreme that they name: placement holds each of 0 .. 63 once.
All inputs are finite; a program needn't handle non-finite values.
Results may differ from a plain program's by a relative error of at most 0.015.
Values may be sent and summed in bfloat16 or wider, within the bound.
No kernel may reach another device: no remote copies, remote signals or barrier semaphores. Data moves between devices by JAX's collectives and lax.ppermute only.
A program may use at most 64 MiB of HBM per device.

v0:
```python
import jax
import jax.numpy as jnp
from jax import lax
from jax.sharding import PartitionSpec as P

HEAD_FEATURES = 128
masked_score = -1e30


def position_lookup(placement, device_ids):
    table = jnp.arange(placement.shape[0], dtype=jnp.int32)
    matches = device_ids[..., None] == table
    return jnp.sum(jnp.where(matches, placement, 0), axis=-1)


def attend(queries, positions, row_groups, placement, placed_keys, placed_values):
    total_rows = queries.shape[0]
    home_rows = placed_keys.shape[0]
    kv_heads = placed_keys.shape[1] // HEAD_FEATURES
    common_across = queries.shape[1] // placed_keys.shape[1]
    group_rows = total_rows // row_groups
    query_grid = queries.reshape(total_rows, kv_heads, common_across, HEAD_FEATURES)
    score_scale = HEAD_FEATURES ** (-0.5)
    initial = tuple(
        (
            (
                jnp.full((kv_heads, common_across, group_rows), masked_score, jnp.float32),
                jnp.zeros((kv_heads, common_across, group_rows), jnp.float32),
                jnp.zeros((kv_heads, common_across, group_rows, HEAD_FEATURES), jnp.float32),
            )
            for member in range(row_groups)
        )
    )

    def update(current, part_queries, part_positions, key_block, value_block, key_positions):
        running_max, running_sum, running_out = current
        scores = (
            jnp.einsum(
                "rkgd,skd->kgrs", part_queries, key_block, preferred_element_type=jnp.float32
            )
            * score_scale
        )
        allowed = key_positions[None, :] <= part_positions[:, None]
        scores = jnp.where(allowed, scores, masked_score)
        new_max = jnp.maximum(running_max, jnp.max(scores, axis=-1))
        weights = jnp.where(allowed, jnp.exp(scores - new_max[..., None]), 0.0)
        shrink = jnp.exp(running_max - new_max)
        new_sum = running_sum * shrink + jnp.sum(weights, axis=-1)
        new_out = running_out * shrink[..., None] + jnp.einsum(
            "kgrs,skd->kgrd",
            weights.astype(jnp.bfloat16),
            value_block,
            preferred_element_type=jnp.float32,
        )
        return (new_max, new_sum, new_out)

    key_piece = lax.all_gather(placed_keys, "ctx", axis=0, tiled=True)
    value_piece = lax.all_gather(placed_values, "ctx", axis=0, tiled=True)
    count = key_piece.shape[0]
    block_count = count // home_rows
    key_grid = key_piece.reshape(block_count, home_rows, kv_heads, HEAD_FEATURES)
    value_grid = value_piece.reshape(block_count, home_rows, kv_heads, HEAD_FEATURES)
    offsets = jnp.arange(block_count, dtype=jnp.int32) * home_rows

    def one_block(states, operands):
        key_block, value_block, block_first = operands
        key_index = block_first + jnp.arange(home_rows, dtype=jnp.int32)
        key_positions = (
            position_lookup(placement, key_index // home_rows) * home_rows + key_index % home_rows
        )
        earliest = jnp.min(key_positions)
        updated = [
            lax.cond(
                earliest <= jnp.max(positions),
                lambda current: update(
                    current, query_grid, positions, key_block, value_block, key_positions
                ),
                lambda current: current,
                states[0],
            )
        ]
        return (tuple(updated), None)

    finished, unused = lax.scan(one_block, initial, (key_grid, value_grid, offsets))
    outputs = [member_state[2] / member_state[1][..., None] for member_state in finished]
    joined = outputs[0]
    return (
        jnp.transpose(joined, (2, 0, 1, 3))
        .reshape(total_rows, queries.shape[1])
        .astype(jnp.bfloat16)
    )


def softmax_mixer(placement, placed_queries, placed_keys, placed_values):
    home_rows = placed_queries.shape[0]
    own_index = lax.axis_index("ctx")
    own_block = position_lookup(placement, own_index)
    positions = own_block * home_rows + jnp.arange(home_rows, dtype=jnp.int32)
    return attend(placed_queries, positions, 1, placement, placed_keys, placed_values)


def body(placement, placed_queries, placed_keys, placed_values, out_weight):
    hidden = softmax_mixer(placement, placed_queries, placed_keys, placed_values)
    partial_sum = jnp.dot(
        hidden,
        lax.all_gather(out_weight, "ctx", axis=1, tiled=True),
        preferred_element_type=jnp.float32,
    )
    rounded_term = lax.optimization_barrier(partial_sum.astype(jnp.bfloat16)).astype(jnp.float32)
    return lax.psum_scatter(
        rounded_term.astype(jnp.bfloat16), "head", scatter_dimension=1, tiled=True
    )


def solution(mesh):
    placed = (P(), P("ctx", "head"), P("ctx", "head"), P("ctx", "head"), P("head", "ctx"))
    return jax.shard_map(
        body, mesh=mesh, in_specs=placed, out_specs=P("ctx", "head"), check_vma=False
    )
```

profile of v0, /device:TPU:22, one launch (start us, length us, event | category | flops | bytes accessed | tf_op | source)
XLA Modules:
  0.0 729.8 jit_solution(3870190778058489720)
XLA Ops:
  12.7 84.4 %all-gather.4.cloned.1.call-done = bf16[16384,128]{1,0:T(8,128)(2,1)} async-done(((bf16[256,128]{1,0:T(8,128)(2,1)}), bf16[16384,128]{1,0:T(8,128)(2,1)}) %all-gather.4.cloned.1.call-update) | async-done | bytes 4194320 | tf_op jit(solution)/shard_map/all_gather | solution.py:57
  97.1 85.2 %all-gather.6.cloned.1.call-done = bf16[16384,128]{1,0:T(8,128)(2,1)} async-done(((bf16[256,128]{1,0:T(8,128)(2,1)}), bf16[16384,128]{1,0:T(8,128)(2,1)}) %all-gather.6.cloned.1.call-update) | async-done | bytes 4194320 | tf_op jit(solution)/shard_map/all_gather | solution.py:58
  182.4 474.6 %while.17 = (s32[]{:T(128)}, f32[1,4,256]{2,1,0:T(4,128)S(1)}, f32[1,4,256]{2,1,0:T(4,128)S(1)}, f32[1,4,256,128]{3,2,1,0:T(8,128)S(1)}, s32[64]{0:T(128)S(1)}, ...) while((s32[]{:T(128)}, f32[1,4,256]{2,1,0:T(4,128)S(1)}, ...), condition=%wide.region_9.10_spmd.clone, body=%wide.region_2.9_spmd.clone.sunk | while | flops 136964864 | bytes 4927015 | solution.py:84
  191.9 2.9 conditional.3
  199.6 2.9 conditional.3
  235.1 2.9 conditional.3
  242.8 2.9 conditional.3
  278.4 2.9 conditional.3
  286.0 2.9 conditional.3
  293.7 2.9 conditional.3
  301.4 2.9 conditional.3
  309.1 2.9 conditional.3
  337.0 2.9 conditional.3
  344.6 2.9 conditional.3
  352.3 2.9 conditional.3
  360.0 2.9 conditional.3
  367.7 2.9 conditional.3
  375.4 2.9 conditional.3
  383.1 2.9 conditional.3
  410.9 2.9 conditional.3
  418.6 2.9 conditional.3
  426.3 2.9 conditional.3
  434.0 2.9 conditional.3
  441.7 2.9 conditional.3
  449.4 2.9 conditional.3
  457.1 2.9 conditional.3
  464.7 2.9 conditional.3
  472.4 2.9 conditional.3
  480.1 2.9 conditional.3
  487.8 2.9 conditional.3
  495.5 2.9 conditional.3
  503.2 2.9 conditional.3
  510.9 2.9 conditional.3
  518.6 2.9 conditional.3
  526.2 2.9 conditional.3
  533.9 2.9 conditional.3
  541.6 2.9 conditional.3
  549.3 2.9 conditional.3
  557.0 2.9 conditional.3
  584.8 2.9 conditional.3
  592.5 2.9 conditional.3
  600.2 2.9 conditional.3
  607.9 2.9 conditional.3
  615.6 2.9 conditional.3
  623.3 2.9 conditional.3
  631.0 2.9 conditional.3
  657.3 4.8 convolution_convert_fusion
  662.1 61.2 %reduce-scatter.2.cloned.1.call-done = bf16[256,512]{1,0:T(8,128)(2,1)} async-done(((bf16[256,4096]{1,0:T(8,128)(2,1)}), bf16[256,512]{1,0:T(8,128)(2,1)}) %reduce-scatter.2.cloned.1.call-update) | async-done | bytes 262160 | tf_op jit(solution)/shard_map/reduce_scatter | solution.py:110
  (824 shorter events, 431.2 us)
Async XLA Ops:
  6.5 90.6 %all-gather.4.cloned.1.call-start = ((), (), s32[]{:S(2)}) async-start(), calls=%async_computation.1 | async-start | bytes 4259840 | tf_op jit(solution)/shard_map/all_gather | solution.py:57
  7.3 175.1 %all-gather.6.cloned.1.call-start = ((), (), s32[]{:S(2)}) async-start(), calls=%async_computation.2 | async-start | bytes 4259840 | tf_op jit(solution)/shard_map/all_gather | solution.py:58
  8.0 649.3 %all-gather.8.cloned.1.call-start = ((), (), s32[]{:S(2)}) async-start(), calls=%async_computation.3 | async-start | bytes 4259840 | tf_op jit(solution)/shard_map/all_gather | solution.py:106
  8.7 714.6 %reduce-scatter.2.cloned.1.call-start = ((), (), s32[]{:S(2)}) async-start(), calls=%async_computation.4 | async-start | bytes 2359296 | tf_op jit(solution)/shard_map/reduce_scatter | solution.py:110
Sparse Core Ops, SparseCore 0:
  10.7 86.3 all-gather.3
  100.5 81.7 all-gather.5
  185.7 82.0 all-gather.7
  662.2 61.0 reduce-scatter.1
where the time goes:
time: 739 us; the launch traced here: 730 us
  waiting for transfers between devices  233 us (32%)
  other arithmetic  196 us (27%)
  matrix products  151 us (20%)
  loops' own time  93.1 us (13%)
  local copies, waits for them, and re-layouts  43.4 us (6%)
  between operations  13.9 us (2%)
    another operation x1, loops' own time, attend(): lax.scan(one_block, initial, (key_grid, value_grid, offsets))  89.6 us
    reduce_min x64, other arithmetic, one_block(): earliest = jnp.min(key_positions)  85.5 us
    all_gather x1, waiting for transfers between devices, attend(): value_piece = lax.all_gather(placed_values, 'ctx', axis=0, tiled=True)  85.2 us
    all_gather x1, waiting for transfers between devices, attend(): key_piece = lax.all_gather(placed_keys, 'ctx', axis=0, tiled=True)  84.4 us
    dot_general x58, matrix products, update(): jnp.einsum('kgrs,skd->kgrd', weights.astype(jnp.bfloat16), value_block, p...  78.1 us
    dot_general x58, matrix products, update(): jnp.einsum('rkgd,skd->kgrs', part_queries, key_block, preferred_element_t...  67.8 us
    reduce_scatter x1, waiting for transfers between devices, body(): lax.psum_scatter(rounded_term.astype(jnp.bfloat16), 'head', scatter_dimen...  61.2 us
    reduce_sum x65, other arithmetic, position_lookup(): return jnp.sum(jnp.where(matches, placement, 0), axis=-1)  49.2 us
  transfers between devices with their start and end apart: 4, of which 3 were waited for; matrix products, arithmetic and copies ran while one was open for 53% of the time, Pallas kernels for 0%

commit v1 on v0

--- a/solution.py
+++ b/solution.py
@@ -54,7 +54,9 @@
         )
         return (new_max, new_sum, new_out)
 
-    key_piece = lax.all_gather(placed_keys, "ctx", axis=0, tiled=True)
+    key_piece = jnp.concatenate(
+        lax.all_to_all(jnp.stack([placed_keys] * lax.axis_size("ctx")), "ctx", 0, 0), axis=0
+    )
     value_piece = lax.all_gather(placed_values, "ctx", axis=0, tiled=True)
     count = key_piece.shape[0]
     block_count = count // home_rows

time: 739 us -> 640 us (0.87)
  the two profiles are of different devices: /device:TPU:22 before, /device:TPU:14 now
where the time goes in v1:
time: 640 us; the launch traced here: 631 us
  waiting for transfers between devices  176 us (28%)
  other arithmetic  149 us (23%)
  matrix products  144 us (22%)
  loops' own time  93 us (15%)
  local copies, waits for them, and re-layouts  44 us (7%)
  between operations  13.9 us (2%)
  starting transfers between devices  11.3 us (2%)
    all_to_all x1, waiting for transfers between devices, attend(): lax.all_to_all(jnp.stack([placed_keys] * lax.axis_size('ctx')), 'ctx', 0, 0)  103 us
    another operation x1, loops' own time, attend(): lax.scan(one_block, initial, (key_grid, value_grid, offsets))  89.6 us
    reduce_min x64, other arithmetic, one_block(): earliest = jnp.min(key_positions)  83.8 us
    dot_general x55, matrix products, update(): jnp.einsum('kgrs,skd->kgrd', weights.astype(jnp.bfloat16), value_block, p...  74.5 us
    reduce_scatter x1, waiting for transfers between devices, body(): lax.psum_scatter(rounded_term.astype(jnp.bfloat16), 'head', scatter_dimen...  71.6 us
    dot_general x55, matrix products, update(): jnp.einsum('rkgd,skd->kgrs', part_queries, key_block, preferred_element_t...  64.3 us
    dynamic_slice x64, local copies, waits for them, and re-layouts, attend(): lax.scan(one_block, initial, (key_grid, value_grid, offsets))  39.3 us
    select_n x64, other arithmetic, one_block(): key_index // home_rows  39.2 us
  transfers between devices with their start and end apart: 4, of which 2 were waited for; matrix products, arithmetic and copies ran while one was open for 53% of the time, Pallas kernels for 0%

profile of v1, /device:TPU:14, one launch (start us, length us, event | category | flops | bytes accessed | tf_op | source)
XLA Modules:
  0.0 631.1 jit_solution(12792474996413105700)
XLA Ops:
  7.3 3.8 stack.2
  11.1 11.2 %all-to-all-start = ((bf16[64,256,128]{2,1,0:T(8,128)(2,1)}), bf16[64,256,128]{2,1,0:T(8,128)(2,1)}, u32[]{:S(2)}, u32[]{:S(2)}) async-start(bf16[64,256,128]{2,1,0:T(8,128)(2,1)} %stack.2), calls=%async_computation | async-start | bytes 8388608 | tf_op jit(solution)/shard_map/all_to_all | solution.py:58
  25.4 102.9 %all-to-all-done = bf16[64,256,128]{2,1,0:T(8,128)(2,1)} async-done(((bf16[64,256,128]{2,1,0:T(8,128)(2,1)}), bf16[64,256,128]{2,1,0:T(8,128)(2,1)}, u32[]{:S(2)}, u32[]{:S(2)}) %all-to-all-start) | async-done | bytes 4194336 | tf_op jit(solution)/shard_map/all_to_all | solution.py:58
  128.4 419.4 %while.17 = (s32[]{:T(128)}, f32[1,4,256]{2,1,0:T(4,128)S(1)}, f32[1,4,256]{2,1,0:T(4,128)S(1)}, f32[1,4,256,128]{3,2,1,0:T(8,128)S(1)}, s32[64]{0:T(128)S(1)}, ...) while((s32[]{:T(128)}, f32[1,4,256]{2,1,0:T(4,128)S(1)}, ...), condition=%wide.region_9.10_spmd.clone, body=%wide.region_2.9_spmd.clone.sunk | while | flops 136964864 | bytes 4927015 | solution.py:86
  136.5 2.9 conditional.3
  143.5 2.9 conditional.3
  158.5 2.9 conditional.3
  165.5 2.9 conditional.3
  172.4 2.9 conditional.3
  179.4 2.9 conditional.3
  190.4 2.9 conditional.3
  197.4 2.9 conditional.3
  204.3 2.9 conditional.3
  211.3 2.9 conditional.3
  218.3 2.9 conditional.3
  225.2 2.9 conditional.3
  239.2 2.9 conditional.3
  257.1 2.9 conditional.3
  275.1 2.9 conditional.3
  282.1 2.9 conditional.3
  289.0 2.9 conditional.3
  296.0 2.9 conditional.3
  314.0 2.9 conditional.3
  327.9 2.9 conditional.3
  341.8 2.9 conditional.3
  348.8 2.9 conditional.3
  355.7 2.9 conditional.3
  362.7 2.9 conditional.3
  376.6 2.9 conditional.3
  383.6 2.9 conditional.3
  390.5 2.9 conditional.3
  397.5 2.9 conditional.3
  411.4 2.9 conditional.3
  418.4 2.9 conditional.3
  425.4 2.9 conditional.3
  432.3 2.9 conditional.3
  446.2 2.9 conditional.3
  453.2 2.9 conditional.3
  460.2 2.9 conditional.3
  475.2 2.9 conditional.3
  496.1 2.9 conditional.3
  503.1 2.9 conditional.3
  510.0 2.9 conditional.3
  530.9 2.9 conditional.3
  537.9 2.9 conditional.3
  544.8 2.9 conditional.3
  548.1 4.8 convolution_convert_fusion
  552.9 71.6 %reduce-scatter.2.cloned.1.call-done = bf16[256,512]{1,0:T(8,128)(2,1)} async-done(((bf16[256,4096]{1,0:T(8,128)(2,1)}), bf16[256,512]{1,0:T(8,128)(2,1)}) %reduce-scatter.2.cloned.1.call-update) | async-done | bytes 262160 | tf_op jit(solution)/shard_map/reduce_scatter | solution.py:112
  (804 shorter events, 368.0 us)
Async XLA Ops:
  6.5 121.8 %all-gather.3.cloned.1.call-start = ((), (), s32[]{:S(2)}) async-start(), calls=%async_computation.2 | async-start | bytes 4259840 | tf_op jit(solution)/shard_map/all_gather | solution.py:60
  11.1 12.0 %copy-start.1 = (s32[64]{0:T(128)S(1)}, s32[64]{0:T(128)}, u32[]{:S(2)}) copy-start(s32[64]{0:T(128)} %param.9) | copy-start | bytes 772
  11.1 14.0 %copy-start = (bf16[256,512]{1,0:T(8,128)(2,1)S(1)}, bf16[256,512]{1,0:T(8,128)(2,1)}, u32[]{:S(2)}) copy-start(bf16[256,512]{1,0:T(8,128)(2,1)} %param.10) | copy-start | bytes 786436
  11.1 117.3 %all-to-all-start = ((bf16[64,256,128]{2,1,0:T(8,128)(2,1)}), bf16[64,256,128]{2,1,0:T(8,128)(2,1)}, u32[]{:S(2)}, u32[]{:S(2)}) async-start(bf16[64,256,128]{2,1,0:T(8,128)(2,1)} %stack.2), calls=%async_computation | async-start | bytes 8388608 | tf_op jit(solution)/shard_map/all_to_all | solution.py:58
  22.3 525.8 %all-gather.5.cloned.1.call-start = ((), (), s32[]{:S(2)}) async-start(), calls=%async_computation.3 | async-start | bytes 4259840 | tf_op jit(solution)/shard_map/all_gather | solution.py:108
  23.0 601.5 %reduce-scatter.2.cloned.1.call-start = ((), (), s32[]{:S(2)}) async-start(), calls=%async_computation.4 | async-start | bytes 2359296 | tf_op jit(solution)/shard_map/reduce_scatter | solution.py:112
Sparse Core Ops, SparseCore 0:
  10.7 102.3 all-gather.2
  116.5 82.7 all-gather.4
  553.1 71.4 reduce-scatter.1
